TPU v7x, 32 devices: a whole 2x2x4 slice. The times are simulated.
32 devices in a mesh: dp: 16 (over z, y, core), tensor: 2 (over x).
Axes of the slice: x: 2, y: 2, z: 4, core: 2. Of those that a mesh axis runs over, the one named last changes fastest.
Arguments:
- tokens: bfloat16 [32, 512, 768], P('dp', 'tensor')
- prob_masks: int32 [2, 32, 12, 512, 40], P(None, 'dp', 'tensor'), may hold values from 0 to 8191, as said below
- branch_masks: int32 [2, 2, 32, 512, 52], P(None, None, 'dp', 'tensor'), may hold values from 0 to 32767, as said below
- attn_weight: float32 [768, 3, 768], P('dp', None, 'tensor'), may hold values from -0.21875 to 0.21875
- attn_first: float32 [768, 3, 768], P('dp', None, 'tensor'), may hold values from -3.0517578e-05 to 3.0517578e-05
- attn_second: float32 [768, 3, 768], P('dp', None, 'tensor'), may hold values from 1.159668e-12 to 1.8615722e-11
- out_weight: float32 [768, 768], P('tensor', 'dp'), may hold values from -0.4375 to 0.4375
- out_first: float32 [768, 768], P('tensor', 'dp'), may hold values from -3.0517578e-05 to 3.0517578e-05
- out_second: float32 [768, 768], P('tensor', 'dp'), may hold values from 1.159668e-12 to 1.8615722e-11
- up_weight: float32 [768, 3072], P('dp', 'tensor'), may hold values from -0.21875 to 0.21875
- up_first: float32 [768, 3072], P('dp', 'tensor'), may hold values from -3.0517578e-05 to 3.0517578e-05
- up_second: float32 [768, 3072], P('dp', 'tensor'), may hold values from 1.159668e-12 to 1.8615722e-11
- down_weight: float32 [3072, 768], P('tensor', 'dp'), may hold values from -0.109375 to 0.109375
- down_first: float32 [3072, 768], P('tensor', 'dp'), may hold values from -3.0517578e-05 to 3.0517578e-05
- down_second: float32 [3072, 768], P('tensor', 'dp'), may hold values from 1.159668e-12 to 1.8615722e-11
- gains: float32 [2, 768], replicated, may hold values from 0.5 to 1.5
- gains_first: float32 [2, 768], replicated, may hold values from -0.00012207031 to 0.00012207031
- gains_second: float32 [2, 768], replicated, may hold values from 1.8615722e-11 to 2.9907227e-10
- shifts: float32 [6, 768], replicated, may hold values from -1.25 to 1.25
- shifts_first: float32 [6, 768], replicated, may hold values from -0.00012207031 to 0.00012207031
- shifts_second: float32 [6, 768], replicated, may hold values from 1.8615722e-11 to 2.9907227e-10
- hidden_bias: float32 [3072], replicated, may hold values from -1.25 to 1.25
- hidden_first: float32 [3072], replicated, may hold values from -0.00012207031 to 0.00012207031
- hidden_second: float32 [3072], replicated, may hold values from 1.8615722e-11 to 2.9907227e-10
Outputs:
- loss: float32 [], replicated
- grad_tokens: float32 [32, 512, 768], P('dp', 'tensor')
- new_attn: float32 [768, 3, 768], P('dp', None, 'tensor')
- new_attn_first: float32 [768, 3, 768], P('dp', None, 'tensor')
- new_attn_second: float32 [768, 3, 768], P('dp', None, 'tensor')
- new_out: float32 [768, 768], P('tensor', 'dp')
- new_out_first: float32 [768, 768], P('tensor', 'dp')
- new_out_second: float32 [768, 768], P('tensor', 'dp')
- new_up: float32 [768, 3072], P('dp', 'tensor')
- new_up_first: float32 [768, 3072], P('dp', 'tensor')
- new_up_second: float32 [768, 3072], P('dp', 'tensor')
- new_down: float32 [3072, 768], P('tensor', 'dp')
- new_down_first: float32 [3072, 768], P('tensor', 'dp')
- new_down_second: float32 [3072, 768], P('tensor', 'dp')
- new_gains: float32 [2, 768], replicated
- new_gains_first: float32 [2, 768], replicated
- new_gains_second: float32 [2, 768], replicated
- new_shifts: float32 [6, 768], replicated
- new_shifts_first: float32 [6, 768], replicated
- new_shifts_second: float32 [6, 768], replicated
- new_hidden: float32 [3072], replicated
- new_hidden_first: float32 [3072], replicated
- new_hidden_second: float32 [3072], replicated
Inputs may be any that keep to these rules, and one draw needn't show every extreme that they name: `prob_masks`: each word holds 13 keep bits for 13 consecutive keys, bit b of word w for key 13 w + b; bits for keys at 512 or past are zero. `branch_masks`: each word holds 15 keep bits for 15 consecutive features, bit b of word w for feature 15 w + b; bits for features at 768 or past are zero.
All inputs are finite; a program needn't handle non-finite values.
Results may differ from a plain program's by a relative error of at most 0.009.
Values may be sent and summed in bfloat16 or wider, within the bound.
No kernel may reach another device: no remote copies, remote signals or barrier semaphores. Data moves between devices by JAX's collectives and lax.ppermute only.
A program may use at most 192 MiB of HBM per device.

v0:
```python
import jax
import jax.numpy as jnp
from jax import lax
from jax.sharding import PartitionSpec as P

HD = 64
STEP = 10
KEEP_SCALE = 1.0 / 0.9


def unpack(packed, length, word_bits):
    places = jnp.arange(word_bits, dtype=jnp.int32)
    bit_flags = jnp.bitwise_and(jnp.right_shift(packed[..., None], places), 1)
    bit_flags = bit_flags.reshape(packed.shape[:-1] + (packed.shape[-1] * word_bits,))
    return bit_flags[..., :length].astype(jnp.float32) * KEEP_SCALE


def layer_norm(values_in, gain_row, shift_row):
    center = values_in - jnp.mean(values_in, axis=-1, keepdims=True)
    spread = jnp.mean(center * center, axis=-1, keepdims=True)
    return center * lax.rsqrt(spread + 1e-12) * gain_row + shift_row


def contrastive(pooled):
    unit_rows = pooled * lax.rsqrt(jnp.sum(pooled * pooled, axis=-1, keepdims=True) + 1e-06)
    logits = jnp.dot(unit_rows[0], unit_rows[1].T, precision=lax.Precision.HIGHEST) * 20.0
    return jnp.mean(jax.nn.logsumexp(logits, axis=1) - jnp.diagonal(logits))


def gelu_exact(values_in):
    return jax.nn.gelu(values_in, approximate=False)


def contract(left_side, right_side, left_dim, right_dim):
    return lax.dot_general(
        left_side,
        right_side,
        (((left_dim,), (right_dim,)), ((), ())),
        preferred_element_type=jnp.float32,
    )


def attend_forward(queries, key_rows, values, prob_words):
    length = queries.shape[0]
    scores = (
        jnp.einsum("qhd,khd->hqk", queries, key_rows, preferred_element_type=jnp.float32) * 0.125
    )
    row_peak = jnp.max(scores, axis=-1, keepdims=True)
    sum_exp = jnp.sum(jnp.exp(scores - row_peak), axis=-1, keepdims=True)
    logsum = row_peak + jnp.log(sum_exp)
    attn_probs = jnp.exp(scores - logsum)
    weighted = (attn_probs[None] * unpack(prob_words, length, 13)).astype(jnp.bfloat16)
    context = jnp.einsum("vhqk,khd->vqhd", weighted, values, preferred_element_type=jnp.float32)
    return (context.astype(jnp.bfloat16).reshape(2, length, -1), logsum[..., 0])


def attend_backward(queries, key_rows, values, prob_words, logsum, grad_context):
    length = queries.shape[0]
    scores = (
        jnp.einsum("qhd,khd->hqk", queries, key_rows, preferred_element_type=jnp.float32) * 0.125
    )
    attn_probs = jnp.exp(scores - logsum[..., None])
    keep_probs = unpack(prob_words, length, 13)
    weighted = (attn_probs[None] * keep_probs).astype(jnp.bfloat16)
    grad_values = jnp.einsum(
        "vhqk,vqhd->khd", weighted, grad_context, preferred_element_type=jnp.float32
    )
    grad_weighted = jnp.einsum(
        "vqhd,khd->vhqk", grad_context, values, preferred_element_type=jnp.float32
    )
    grad_probs = jnp.sum(grad_weighted * keep_probs, axis=0)
    inner = jnp.sum(grad_probs * attn_probs, axis=-1, keepdims=True)
    grad_scores = (attn_probs * (grad_probs - inner)).astype(jnp.bfloat16)
    grad_queries = (
        jnp.einsum("hqk,khd->qhd", grad_scores, key_rows, preferred_element_type=jnp.float32)
        * 0.125
    )
    grad_keys = (
        jnp.einsum("hqk,qhd->khd", grad_scores, queries, preferred_element_type=jnp.float32) * 0.125
    )
    return jnp.stack([grad_queries, grad_keys, grad_values], axis=1)


def adam_direction(weight, gradient, first_moment, second, decay_rate):
    new_first = 0.9 * first_moment + 0.1 * gradient
    new_second = 0.999 * second + 0.001 * gradient * gradient
    first_hat = new_first / (1.0 - 0.9**STEP)
    second_hat = new_second / (1.0 - 0.999**STEP)
    update = first_hat / (jnp.sqrt(second_hat) + 1e-06) + decay_rate * weight
    return (new_first, new_second, update)


def small_step(weight, gradient, first_moment, second):
    new_first, new_second, update = adam_direction(weight, gradient, first_moment, second, 0.0)
    trust_ratio = jnp.sqrt(jnp.sum(weight * weight, axis=-1, keepdims=True)) / jnp.sqrt(
        jnp.sum(update * update, axis=-1, keepdims=True)
    )
    return (weight - 0.25 * trust_ratio * update, new_first, new_second)


def shards(
    tokens,
    prob_masks,
    branch_masks,
    attn_weight,
    attn_first,
    attn_second,
    out_weight,
    out_first,
    out_second,
    up_weight,
    up_first,
    up_second,
    down_weight,
    down_first,
    down_second,
    gains,
    gains_first,
    gains_second,
    shifts,
    shifts_first,
    shifts_second,
    hidden_bias,
    hidden_first,
    hidden_second,
):
    tensor_count = lax.axis_size("tensor")
    tensor_rank = lax.axis_index("tensor")
    data_count = lax.axis_size("dp")
    data_rank = lax.axis_index("dp")
    seq_local, half_len, model_width = tokens.shape
    seq_len = half_len * tensor_count
    heads_local = prob_masks.shape[2]
    local_width = heads_local * HD
    hidden_local = up_weight.shape[1]
    scale_loss = 64.0 * data_count * seq_local * seq_len
    attn_low, out_low, up_low, down_low = (
        lax.all_gather(attn_weight.astype(jnp.bfloat16), "dp", axis=0, tiled=True),
        lax.all_gather(out_weight.astype(jnp.bfloat16), "dp", axis=1, tiled=True),
        lax.all_gather(up_weight.astype(jnp.bfloat16), "dp", axis=0, tiled=True),
        lax.all_gather(down_weight.astype(jnp.bfloat16), "dp", axis=1, tiled=True),
    )
    token_full = lax.all_gather(tokens, "tensor", axis=1, tiled=True)
    token_flat = token_full.reshape(seq_local * seq_len, model_width)
    attn_matrix = attn_low.reshape(model_width, 3 * local_width)
    bias_query = lax.dynamic_slice_in_dim(shifts[0], tensor_rank * local_width, local_width)
    bias_value = lax.dynamic_slice_in_dim(shifts[1], tensor_rank * local_width, local_width)
    qkv_bias = jnp.stack([bias_query, jnp.zeros_like(bias_query), bias_value])
    projected = (
        jnp.dot(token_flat, attn_matrix, preferred_element_type=jnp.float32).reshape(
            seq_local, seq_len, 3, local_width
        )
        + qkv_bias
    )
    qkv_low = projected.astype(jnp.bfloat16)
    heads_shape = (seq_local, seq_len, heads_local, HD)
    queries = qkv_low[:, :, 0].reshape(heads_shape)
    key_rows = qkv_low[:, :, 1].reshape(heads_shape)
    values = qkv_low[:, :, 2].reshape(heads_shape)
    mask_words = jnp.moveaxis(prob_masks, 1, 0)
    context, logsum = lax.map(
        lambda sequence_items: attend_forward(*sequence_items),
        (queries, key_rows, values, mask_words),
    )
    context_flat = jnp.moveaxis(context, 1, 0).reshape(-1, local_width)
    attn_part = jnp.dot(context_flat, out_low, preferred_element_type=jnp.float32).reshape(
        2, seq_local, seq_len, model_width
    )
    attn_out = (
        lax.psum_scatter(
            attn_part.astype(jnp.bfloat16), "tensor", scatter_dimension=2, tiled=True
        ).astype(jnp.float32)
        + shifts[2]
    )
    keep_attn = unpack(branch_masks[0], model_width, 15)
    keep_ffn = unpack(branch_masks[1], model_width, 15)
    first_in = tokens.astype(jnp.float32)[None] + attn_out * keep_attn
    normed, norm_one_back = jax.vjp(layer_norm, first_in, gains[0], shifts[3])
    normed_full = lax.all_gather(normed.astype(jnp.bfloat16), "tensor", axis=2, tiled=True)
    normed_flat = normed_full.reshape(-1, model_width)
    bias_hidden = lax.dynamic_slice_in_dim(hidden_bias, tensor_rank * hidden_local, hidden_local)
    hidden_pre = jnp.dot(normed_flat, up_low, preferred_element_type=jnp.float32) + bias_hidden
    gelu_value, gelu_back = jax.vjp(gelu_exact, hidden_pre)
    active = gelu_value.astype(jnp.bfloat16)
    ffn_part = jnp.dot(active, down_low, preferred_element_type=jnp.float32).reshape(
        2, seq_local, seq_len, model_width
    )
    ffn_out = (
        lax.psum_scatter(
            ffn_part.astype(jnp.bfloat16), "tensor", scatter_dimension=2, tiled=True
        ).astype(jnp.float32)
        + shifts[4]
    )
    output, norm_two_back = jax.vjp(layer_norm, normed + ffn_out * keep_ffn, gains[1], shifts[5])
    pooled_part = jnp.sum(output, axis=2) / seq_len
    pooled_all = lax.all_gather(pooled_part, ("dp", "tensor"), axis=1, tiled=True)
    pooled = (
        pooled_all.reshape(2, data_count, tensor_count, seq_local, model_width)
        .sum(axis=2)
        .reshape(2, data_count * seq_local, model_width)
    )
    loss_value, loss_back = jax.vjp(contrastive, pooled)
    grad_pooled = loss_back(jnp.float32(scale_loss))[0]
    grad_own = lax.dynamic_slice_in_dim(grad_pooled, data_rank * seq_local, seq_local, axis=1)
    grad_output = jnp.broadcast_to((grad_own / seq_len)[:, :, None, :], output.shape)
    grad_second, grad_gain_two, grad_shift_two = norm_two_back(grad_output)
    grad_ffn = (grad_second * keep_ffn).astype(jnp.bfloat16)
    grad_ffn_full = lax.all_gather(grad_ffn, "tensor", axis=2, tiled=True)
    grad_ffn_flat = grad_ffn_full.reshape(-1, model_width)
    grad_down = contract(active, grad_ffn_flat, 0, 0)
    grad_active = contract(grad_ffn_flat, down_low, 1, 1)
    grad_hidden = gelu_back(grad_active)[0].astype(jnp.bfloat16)
    grad_up = contract(normed_flat, grad_hidden, 0, 0)
    normed_back = contract(grad_hidden, up_low, 1, 1).reshape(2, seq_local, seq_len, model_width)
    grad_normed = grad_second + lax.psum_scatter(
        normed_back.astype(jnp.bfloat16), "tensor", scatter_dimension=2, tiled=True
    ).astype(jnp.float32)
    grad_first, grad_gain_one, grad_shift_one = norm_one_back(grad_normed)
    grad_attn = (grad_first * keep_attn).astype(jnp.bfloat16)
    grad_attn_full = lax.all_gather(grad_attn, "tensor", axis=2, tiled=True)
    grad_attn_flat = grad_attn_full.reshape(-1, model_width)
    grad_out = contract(context_flat, grad_attn_flat, 0, 0)
    grad_context = (
        contract(grad_attn_flat, out_low, 1, 1)
        .astype(jnp.bfloat16)
        .reshape(2, seq_local, seq_len, heads_local, HD)
    )
    grad_qkv = lax.map(
        lambda sequence_items: attend_backward(*sequence_items),
        (queries, key_rows, values, mask_words, logsum, jnp.moveaxis(grad_context, 1, 0)),
    )
    qkv_grad_low = grad_qkv.reshape(seq_local * seq_len, 3 * local_width).astype(jnp.bfloat16)
    grad_attn_weight = contract(token_flat, qkv_grad_low, 0, 0).reshape(model_width, 3, local_width)
    attn_reduced, out_reduced, up_reduced, down_reduced = (
        lax.psum_scatter(grad_attn_weight, "dp", scatter_dimension=0, tiled=True),
        lax.psum_scatter(grad_out, "dp", scatter_dimension=1, tiled=True),
        lax.psum_scatter(grad_up, "dp", scatter_dimension=0, tiled=True),
        lax.psum_scatter(grad_down, "dp", scatter_dimension=1, tiled=True),
    )
    token_back = contract(qkv_grad_low, attn_matrix, 1, 1).reshape(seq_local, seq_len, model_width)
    grad_tokens = lax.psum_scatter(
        token_back.astype(jnp.bfloat16), "tensor", scatter_dimension=1, tiled=True
    ).astype(jnp.float32) + jnp.sum(grad_first, axis=0)
    qkv_sums = jnp.sum(qkv_grad_low.astype(jnp.float32).reshape(-1, 3, local_width), axis=0)
    zero_row = jnp.zeros((model_width,), jnp.float32)
    query_row = lax.dynamic_update_slice_in_dim(zero_row, qkv_sums[0], tensor_rank * local_width, 0)
    value_row = lax.dynamic_update_slice_in_dim(zero_row, qkv_sums[2], tensor_rank * local_width, 0)
    shift_grads = jnp.stack(
        [
            query_row,
            value_row,
            jnp.sum(grad_attn.astype(jnp.float32), axis=(0, 1, 2)),
            grad_shift_one,
            jnp.sum(grad_ffn.astype(jnp.float32), axis=(0, 1, 2)),
            grad_shift_two,
        ]
    )
    gain_grads = jnp.stack([grad_gain_one, grad_gain_two])
    hidden_grads = lax.dynamic_update_slice_in_dim(
        jnp.zeros((hidden_local * tensor_count,), jnp.float32),
        jnp.sum(grad_hidden.astype(jnp.float32), axis=0),
        tensor_rank * hidden_local,
        0,
    )
    attn_new_first, attn_new_second, attn_update = adam_direction(
        attn_weight, attn_reduced / scale_loss, attn_first, attn_second, 0.01
    )
    out_new_first, out_new_second, out_update = adam_direction(
        out_weight, out_reduced / scale_loss, out_first, out_second, 0.01
    )
    up_new_first, up_new_second, up_update = adam_direction(
        up_weight, up_reduced / scale_loss, up_first, up_second, 0.01
    )
    down_new_first, down_new_second, down_update = adam_direction(
        down_weight, down_reduced / scale_loss, down_first, down_second, 0.01
    )
    squares = jnp.concatenate(
        [
            jnp.sum(attn_weight * attn_weight, axis=(0, 2)),
            jnp.stack(
                [
                    jnp.sum(out_weight * out_weight),
                    jnp.sum(up_weight * up_weight),
                    jnp.sum(down_weight * down_weight),
                ]
            ),
            jnp.sum(attn_update * attn_update, axis=(0, 2)),
            jnp.stack(
                [
                    jnp.sum(out_update * out_update),
                    jnp.sum(up_update * up_update),
                    jnp.sum(down_update * down_update),
                ]
            ),
        ]
    )
    summed_squares, gain_total, shift_total, hidden_total = lax.psum(
        (squares, gain_grads, shift_grads, hidden_grads), ("dp", "tensor")
    )
    trust_ratio = jnp.sqrt(summed_squares[:6]) / jnp.sqrt(summed_squares[6:])
    new_attn = attn_weight - 0.25 * trust_ratio[0:3][None, :, None] * attn_update
    new_out = out_weight - 0.25 * trust_ratio[3] * out_update
    new_up = up_weight - 0.25 * trust_ratio[4] * up_update
    new_down = down_weight - 0.25 * trust_ratio[5] * down_update
    new_gains, new_gains_first, new_gains_second = small_step(
        gains, gain_total / scale_loss, gains_first, gains_second
    )
    new_shifts, new_shifts_first, new_shifts_second = small_step(
        shifts, shift_total / scale_loss, shifts_first, shifts_second
    )
    new_hidden, new_hidden_first, new_hidden_second = small_step(
        hidden_bias, hidden_total / scale_loss, hidden_first, hidden_second
    )
    return (
        loss_value,
        grad_tokens,
        new_attn,
        attn_new_first,
        attn_new_second,
        new_out,
        out_new_first,
        out_new_second,
        new_up,
        up_new_first,
        up_new_second,
        new_down,
        down_new_first,
        down_new_second,
        new_gains,
        new_gains_first,
        new_gains_second,
        new_shifts,
        new_shifts_first,
        new_shifts_second,
        new_hidden,
        new_hidden_first,
        new_hidden_second,
    )


def solution(mesh):
    return jax.shard_map(
        shards,
        mesh=mesh,
        in_specs=(
            P("dp", "tensor", None),
            P(None, "dp", "tensor", None, None),
            P(None, None, "dp", "tensor", None),
            P("dp", None, "tensor"),
            P("dp", None, "tensor"),
            P("dp", None, "tensor"),
            P("tensor", "dp"),
            P("tensor", "dp"),
            P("tensor", "dp"),
            P("dp", "tensor"),
            P("dp", "tensor"),
            P("dp", "tensor"),
            P("tensor", "dp"),
            P("tensor", "dp"),
            P("tensor", "dp"),
            P(),
            P(),
            P(),
            P(),
            P(),
            P(),
            P(),
            P(),
            P(),
        ),
        out_specs=(
            P(),
            P("dp", "tensor", None),
            P("dp", None, "tensor"),
            P("dp", None, "tensor"),
            P("dp", None, "tensor"),
            P("tensor", "dp"),
            P("tensor", "dp"),
            P("tensor", "dp"),
            P("dp", "tensor"),
            P("dp", "tensor"),
            P("dp", "tensor"),
            P("tensor", "dp"),
            P("tensor", "dp"),
            P("tensor", "dp"),
            P(),
            P(),
            P(),
            P(),
            P(),
            P(),
            P(),
            P(),
            P(),
        ),
        check_vma=False,
    )
```

profile of v0, /device:TPU:0, one launch (start us, length us, event | category | flops | bytes accessed | tf_op | source)
XLA Modules:
  0.0 1080.3 jit_solution(10038383568165098798)
XLA Ops:
  14.4 27.1 %all_gather.29 = bf16[384,768]{0,1:T(8,128)(2,1)} all-gather(bf16[384,48]{0,1:T(8,128)(2,1)S(1)} %convert_element_type.122), channel_id=1, replica_groups=mesh['dp'=16,'tensor'=2] {'dp'}, dimensions={1}, use_global_device_ids=true | all-gather | bytes 626688 | tf_op jit(solution)/shard_map/all_gather | solution.py:139
  41.6 13.7 %all-gather.10.cloned.1.call-done = bf16[768,3,384]{2,0,1:T(8,128)(2,1)} async-done(((bf16[48,3,384]{2,0,1:T(8,128)(2,1)}), bf16[768,3,384]{2,0,1:T(8,128)(2,1)}) %all-gather.10.cloned.1.call-update) | async-done | bytes 1769488 | tf_op jit(solution)/shard_map/all_gather | solution.py:138
  55.3 3.9 copy.163
  59.1 23.8 %all-gather.8.cloned.1.call-done = bf16[2,512,768]{2,1,0:T(8,128)(2,1)} async-done(((bf16[2,256,768]{2,1,0:T(8,128)(2,1)}), bf16[2,512,768]{2,1,0:T(8,128)(2,1)}) %all-gather.8.cloned.1.call-update) | async-done | bytes 1572880 | tf_op jit(solution)/shard_map/all_gather | solution.py:143
  83.0 4.0 add_convert_fusion.1
  88.1 108.0 %while.22 = (s32[]{:T(128)}, bf16[2,2,512,384]{2,3,1,0:T(8,128)(2,1)}, f32[2,6,512]{2,1,0:T(8,128)}, bf16[2,512,6,64]{1,3,2,0:T(8,128)(2,1)}, s32[2,2,6,512,40]{...) while((s32[]{:T(128)}, ...), condition=%wide.region_3.4_spmd, body=%wide.region_0.3_spmd.sunk | while | flops 632681472 | bytes 140713456 | solution.py:161
  88.4 3.6 shift_right_arithmetic.162
  92.0 6.3 slice.162
  98.3 19.0 %copy.239 = s32[2,6,512,512]{3,2,1,0:T(8,128)} copy(s32[2,6,512,512]{2,0,3,1:T(2,128)} %slice.162) | data formatting | bytes 25165824 | tf_op jit(solution)/shard_map/while
  121.6 3.7 exponential_multiply_fusion.2
  125.2 6.6 copy.240
  131.9 8.9 fusion.134
  142.4 3.6 shift_right_arithmetic.162
  146.0 6.3 slice.162
  152.3 19.0 %copy.239 = s32[2,6,512,512]{3,2,1,0:T(8,128)} copy(s32[2,6,512,512]{2,0,3,1:T(2,128)} %slice.162) | data formatting | bytes 25165824 | tf_op jit(solution)/shard_map/while
  175.6 3.7 exponential_multiply_fusion.2
  179.2 6.6 copy.240
  185.8 8.9 fusion.134
  196.1 6.3 convolution_convert_fusion.3
  204.2 9.9 all-gather.12.cloned.1.call-start
  220.5 4.1 copy.202
  224.6 21.2 %reduce-scatter.9.cloned.1.call-done = bf16[2,2,256,768]{3,2,1,0:T(8,128)(2,1)} async-done(((bf16[2,2,512,768]{3,2,1,0:T(8,128)(2,1)}), bf16[2,2,256,768]{3,2,1,0:T(8,128)(2,1)}) %reduce-scatter.9.cloned.1.call-update) | async-done | bytes 1572880 | tf_op jit(solution)/shard_map/reduce_scatter | solution.py:170
  253.1 37.9 %all-gather.14.cloned.1.call-done = bf16[768,1536]{1,0:T(8,128)(2,1)} async-done(((bf16[48,1536]{1,0:T(8,128)(2,1)}), bf16[768,1536]{1,0:T(8,128)(2,1)}) %all-gather.14.cloned.1.call-update) | async-done | bytes 2359312 | tf_op jit(solution)/shard_map/all_gather | solution.py:140
  291.1 45.2 %all-gather.12.cloned.1.call-done = bf16[2,2,512,768]{3,2,1,0:T(8,128)(2,1)} async-done(((bf16[2,2,256,768]{3,2,1,0:T(8,128)(2,1)}), bf16[2,2,512,768]{3,2,1,0:T(8,128)(2,1)}) %all-gather.12.cloned.1.call-update) | async-done | bytes 3145744 | tf_op jit(solution)/shard_map/all_gather | solution.py:179
  336.3 34.9 %multiply_convert_fusion.6 = (bf16[2048,1536]{1,0:T(8,128)(2,1)}, f32[2048,1536]{1,0:T(8,128)}, f32[2048,1536]{1,0:T(8,128)}) fusion(f32[1536]{0:T(1024)S(1)} %dynamic_slice.48, bf16[2048,768]{1,0:T(8,128)(2,1)} %bitcast.269, bf16[768,1536]{1,0:T(8,128)(2,1)} %all-gather.14.cloned.1.call-done), kind=kOutput, calls=%fused_computation.68 | convolution fusion | flops 5039456256 | bytes 36968448 | tf_op jit(solution)/shard_map/dot_general | solution.py:182
  371.2 10.4 all-gather.16.cloned.1.call-done
  381.5 9.1 convolution_convert_fusion.1
  392.8 3.6 copy.203
  396.9 36.0 %reduce-scatter.11.cloned.1.call-done = bf16[2,2,256,768]{3,2,1,0:T(8,128)(2,1)} async-done(((bf16[2,2,512,768]{3,2,1,0:T(8,128)(2,1)}), bf16[2,2,256,768]{3,2,1,0:T(8,128)(2,1)}) %reduce-scatter.11.cloned.1.call-update) | async-done | bytes 1572880 | tf_op jit(solution)/shard_map/reduce_scatter | solution.py:189
  433.0 4.1 fusion.84
  438.9 74.0 %all_gather.33 = f32[2,64,768]{2,0,1:T(2,128)} all-gather(f32[2,2,768]{2,0,1:T(2,128)S(1)} %copy.168), channel_id=1, replica_groups=mesh['dp'=16,'tensor'=2] {'dp','tensor'}, dimensions={1}, use_global_device_ids=true | all-gather | bytes 405504 | tf_op jit(solution)/shard_map/all_gather | solution.py:196
  535.5 40.5 %all-gather.18.cloned.1.call-done = bf16[2,2,512,768]{3,2,1,0:T(8,128)(2,1)} async-done(((bf16[2,2,256,768]{3,2,1,0:T(8,128)(2,1)}), bf16[2,2,512,768]{3,2,1,0:T(8,128)(2,1)}) %all-gather.18.cloned.1.call-update) | async-done | bytes 3145744 | tf_op jit(solution)/shard_map/all_gather | solution.py:208
  576.1 17.6 %convert_reduce_fusion = (f32[1536]{0:T(1024)}, bf16[2048,1536]{1,0:T(8,128)(2,1)S(1)}) fusion(f32[2048,1536]{1,0:T(8,128)} %get-tuple-element.243, bf16[2048,768]{1,0:T(8,128)(2,1)} %bitcast.271, bf16[1536,768]{0,1:T(8,128)(2,1)} %all-gather.16.cloned.1.call-done, f32[2048,1536]{1,0:T(8,128)} %get-tuple-element.270, f32[1536]{0:T(1024)S(1)} %copy-done.87), kind=kOutput, calls=%fused_computation.66 | convolution fusion | flops 4885314048 | bytes 36974592 | tf_op jit(solution)/shard_map/dot_general | solution.py:35
  593.6 6.5 convolution_convert_fusion
  600.3 43.4 %reduce-scatter.13.cloned.1.call-done = bf16[2,2,256,768]{3,2,1,0:T(8,128)(2,1)} async-done(((bf16[2,2,512,768]{3,2,1,0:T(8,128)(2,1)}), bf16[2,2,256,768]{3,2,1,0:T(8,128)(2,1)}) %reduce-scatter.13.cloned.1.call-update) | async-done | bytes 1572880 | tf_op jit(solution)/shard_map/reduce_scatter | solution.py:215
  643.7 5.0 multiply_reduce_fusion.3
  651.3 3.3 convert_reduce_fusion.3
  654.7 9.6 fusion.92
  666.4 9.5 fusion.93
  676.1 23.6 %all-gather.20.cloned.1.call-done = bf16[2,2,512,768]{3,2,1,0:T(8,128)(2,1)} async-done(((bf16[2,2,256,768]{3,2,1,0:T(8,128)(2,1)}), bf16[2,2,512,768]{3,2,1,0:T(8,128)(2,1)}) %all-gather.20.cloned.1.call-update) | async-done | bytes 3145744 | tf_op jit(solution)/shard_map/all_gather | solution.py:220
  699.7 3.7 convolution_convert_fusion.2
  707.8 4.5 convolution_bitcast_fusion
  712.6 93.9 %while.23 = (s32[]{:T(128)}, bf16[2,512,3,6,64]{1,4,3,2,0:T(8,128)(2,1)}, bf16[2,512,6,64]{1,3,2,0:T(8,128)(2,1)S(1)}, bf16[2,512,6,64]{1,3,2,0:T(8,128)(2,1)}, ...) while((s32[]{:T(128)}, ...), condition=%wide.region_26.27_spmd, body=%wide.region_23.26_spmd.sunk | while | flops 1462367232 | bytes 228946432 | solution.py:228
  713.0 3.6 shift_right_arithmetic.169
  716.6 6.3 slice.164
  723.0 12.5 %fusion.142 = f32[6,512,512]{1,2,0:T(8,128)} fusion(s32[2,6,512,512]{2,0,3,1:T(2,128)} %slice.164, s32[512]{0:T(512)S(1)} %slice.165, bf16[2,2,512,6,64]{2,4,1,3,0:T(8,128)(2,1)} %get-tuple-element.435, s32[]{:T(128)S(6)} %copy.259, bf16[2,512,6,64]{1,3,2,0:T(8,128)(2,1)} %get-tuple-element.434), kind=kOutput, calls=%fused_computation.27.clone.1 | convolution fusion | flops 419954688 | bytes 20057088 | tf_op jit(solution)/shard_map/while/body/eval_jaxpr/vqhd,khd->vhqk/dot_general | solution.py:68
  735.6 4.8 multiply_reduce_fusion.25
  740.4 5.6 multiply_convert_fusion.18
  747.3 6.1 fusion.143
  759.4 3.6 shift_right_arithmetic.169
  763.0 6.3 slice.164
  769.4 12.4 %fusion.142 = f32[6,512,512]{1,2,0:T(8,128)} fusion(s32[2,6,512,512]{2,0,3,1:T(2,128)} %slice.164, s32[512]{0:T(512)S(1)} %slice.165, bf16[2,2,512,6,64]{2,4,1,3,0:T(8,128)(2,1)} %get-tuple-element.435, s32[]{:T(128)S(6)} %copy.259, bf16[2,512,6,64]{1,3,2,0:T(8,128)(2,1)} %get-tuple-element.434), kind=kOutput, calls=%fused_computation.27.clone.1 | convolution fusion | flops 419954688 | bytes 20057088 | tf_op jit(solution)/shard_map/while/body/eval_jaxpr/vqhd,khd->vhqk/dot_general | solution.py:68
  781.8 4.8 multiply_reduce_fusion.25
  786.7 5.9 multiply_convert_fusion.18
  793.9 6.3 fusion.143
  800.3 3.4 fusion.144
  806.5 4.1 copy.178
  818.7 5.0 convolution_convert_fusion.4
  829.9 28.2 %reduce-scatter.23.cloned.1.call-done = f32[1536,48]{0,1:T(8,128)} async-done(((f32[1536,768]{0,1:T(8,128)}), f32[1536,48]{0,1:T(8,128)}) %reduce-scatter.23.cloned.1.call-update) | async-done | bytes 294928 | tf_op jit(solution)/shard_map/reduce_scatter | solution.py:238
  862.3 56.9 %reduce-scatter.19.cloned.1.call-done = f32[384,48]{0,1:T(8,128)} async-done(((f32[384,768]{0,1:T(8,128)}), f32[384,48]{0,1:T(8,128)}) %reduce-scatter.19.cloned.1.call-update) | async-done | bytes 73744 | tf_op jit(solution)/shard_map/reduce_scatter | solution.py:236
  920.8 69.6 %reduce-scatter.17.cloned.1.call-done = f32[48,3,384]{2,0,1:T(8,128)} async-done(((f32[768,3,384]{2,0,1:T(8,128)}), f32[48,3,384]{2,0,1:T(8,128)}) %reduce-scatter.17.cloned.1.call-update) | async-done | bytes 221200 | tf_op jit(solution)/shard_map/reduce_scatter | solution.py:235
  991.9 4.0 concatenate.8
  995.9 22.3 %reduce-scatter.15.cloned.1.call-done = bf16[2,256,768]{2,1,0:T(8,128)(2,1)} async-done(((bf16[2,512,768]{2,1,0:T(8,128)(2,1)}), bf16[2,256,768]{2,1,0:T(8,128)(2,1)}) %reduce-scatter.15.cloned.1.call-update) | async-done | bytes 786448 | tf_op jit(solution)/shard_map/reduce_scatter | solution.py:241
  1021.1 40.1 %all-reduce.2 = (f32[12]{0:T(128)S(1)}, f32[2,768]{1,0:T(2,128)S(1)}, f32[6,768]{1,0:T(8,128)S(1)}, f32[3072]{0:T(1024)S(1)}) all-reduce(f32[12]{0:T(128)S(1)} %concatenate.8, f32[2,768]{1,0:T(2,128)S(1)} %copy-done.71, f32[6,768]{1,0:T(8,128)S(1)} %stack.81, ...), channel_id=1, replica_groups=mesh['dp'=16,'tensor'=2] {'dp','tensor'}, use_global_device_ids=true, to_apply=%region_41.42 | all-reduce | flops 9228 | bytes 73824 | tf_op jit(solution)/shard_map/psum | solution.py:297
  (415 shorter events, 114.4 us)
Async XLA Ops:
  7.2 48.1 %all-gather.10.cloned.1.call-start = ((), (), s32[]{:S(2)}) async-start(), calls=%async_computation.9 | async-start | bytes 1880064 | tf_op jit(solution)/shard_map/all_gather | solution.py:138
  8.9 74.1 %all-gather.8.cloned.1.call-start = ((), (), s32[]{:S(2)}) async-start(), calls=%async_computation.8 | async-start | bytes 2359296 | tf_op jit(solution)/shard_map/all_gather | solution.py:143
  9.6 236.2 %reduce-scatter.9.cloned.1.call-start = ((), (), s32[]{:S(2)}) async-start(), calls=%async_computation.10 | async-start | bytes 4718592 | tf_op jit(solution)/shard_map/reduce_scatter | solution.py:170
  131.9 9.0 copy-start.97
  185.8 9.0 copy-start.97
  202.4 88.7 %all-gather.14.cloned.1.call-start = ((), (), s32[]{:S(2)}) async-start(), calls=%async_computation.12 | async-start | bytes 2506752 | tf_op jit(solution)/shard_map/all_gather | solution.py:140
  202.4 14.3 %copy-start.31 = (s32[2,2,2,256,52]{3,2,4,1,0:T(2,128)S(1)}, s32[2,2,2,256,52]{3,2,4,1,0:T(2,128)}, u32[]{:S(2)}) copy-start(s32[2,2,2,256,52]{3,2,4,1,0:T(2,128)} %param.30) | copy-start | bytes 1277956
  204.2 132.1 %all-gather.12.cloned.1.call-start = ((), (), s32[]{:S(2)}) async-start(), calls=%async_computation.11 | async-start | bytes 4718592 | tf_op jit(solution)/shard_map/all_gather | solution.py:179
  216.7 216.2 %copy-start.50 = (s32[780]{0:T(1024)}, s32[780]{0:T(1024)S(1)}, u32[]{:S(2)}) copy-start(s32[780]{0:T(1024)S(1)} %shift_right_arithmetic.92) | copy-start | bytes 9364
  220.5 25.4 %copy-start.72 = (f32[768]{0:T(1024)S(1)}, f32[768]{0:T(1024)}, u32[]{:S(2)}) copy-start(f32[768]{0:T(1024)} %get-tuple-element.176) | copy-start | bytes 9220
  224.6 24.2 %copy-start.12 = (s32[2,2,256,768]{3,2,1,0:T(8,128)}, s32[2,2,256,768]{3,2,1,0:T(8,128)S(1)}, u32[]{:S(2)}) copy-start(s32[2,2,256,768]{3,2,1,0:T(8,128)S(1)} %copy.202) | copy-start | bytes 9437188
  224.6 208.3 %copy-start.52 = (f32[768]{0:T(1024)}, f32[768]{0:T(1024)S(1)}, u32[]{:S(2)}) copy-start(f32[768]{0:T(1024)S(1)} %get-tuple-element.181) | copy-start | bytes 9220
  224.6 213.6 %copy-start.40 = (f32[768]{0:T(1024)}, f32[768]{0:T(1024)S(1)}, u32[]{:S(2)}) copy-start(f32[768]{0:T(1024)S(1)} %get-tuple-element.180) | copy-start | bytes 9220
  248.8 184.1 %copy-start.45 = (f32[2,2,256]{2,1,0:T(2,128)}, f32[2,2,256]{2,1,0:T(2,128)S(1)}, u32[]{:S(2)}) copy-start(f32[2,2,256]{2,1,0:T(2,128)S(1)} %broadcast_multiply_fusion.3) | copy-start | bytes 12292
  249.4 183.6 %copy-start.54 = (f32[2,2,256]{2,1,0:T(2,128)}, f32[2,2,256]{2,1,0:T(2,128)S(1)}, u32[]{:S(2)}) copy-start(f32[2,2,256]{2,1,0:T(2,128)S(1)} %fusion.71) | copy-start | bytes 12292
  252.2 129.3 %all-gather.16.cloned.1.call-start = ((), (), s32[]{:S(2)}) async-start(), calls=%async_computation.13 | async-start | bytes 2506752 | tf_op jit(solution)/shard_map/all_gather | solution.py:141
  253.0 179.9 %reduce-scatter.11.cloned.1.call-start = ((), (), s32[]{:S(2)}) async-start(), calls=%async_computation.14 | async-start | bytes 4718592 | tf_op jit(solution)/shard_map/reduce_scatter | solution.py:189
  253.1 118.0 %copy-start.86 = (f32[1536]{0:T(1024)}, f32[1536]{0:T(1024)S(1)}, u32[]{:S(2)}) copy-start(f32[1536]{0:T(1024)S(1)} %dynamic_slice.48) | copy-start | bytes 18436
  390.6 185.4 %all-gather.18.cloned.1.call-start = ((), (), s32[]{:S(2)}) async-start(), calls=%async_computation.15 | async-start | bytes 4718592 | tf_op jit(solution)/shard_map/all_gather | solution.py:208
  392.8 40.1 %copy-start.75 = (f32[768]{0:T(1024)S(1)}, f32[768]{0:T(1024)}, u32[]{:S(2)}) copy-start(f32[768]{0:T(1024)} %get-tuple-element.174) | copy-start | bytes 9220
  437.6 77.0 %copy-start.47 = (f32[2,2,256]{2,1,0:T(2,128)}, f32[2,2,256]{2,1,0:T(2,128)S(1)}, u32[]{:S(2)}) copy-start(f32[2,2,256]{2,1,0:T(2,128)S(1)} %fusion.72) | copy-start | bytes 12292
  532.1 44.0 %copy-start.87 = (f32[1536]{0:T(1024)S(1)}, f32[1536]{0:T(1024)}, u32[]{:S(2)}) copy-start(f32[1536]{0:T(1024)} %copy-done.86) | copy-start | bytes 18436
  535.1 108.6 %reduce-scatter.13.cloned.1.call-start = ((), (), s32[]{:S(2)}) async-start(), calls=%async_computation.16 | async-start | bytes 4718592 | tf_op jit(solution)/shard_map/reduce_scatter | solution.py:215
  576.0 17.6 %copy-start.95 = (bf16[768,1536]{1,0:T(8,128)(2,1)S(1)}, bf16[768,1536]{1,0:T(8,128)(2,1)}, u32[]{:S(2)}) copy-start(bf16[768,1536]{1,0:T(8,128)(2,1)} %all-gather.14.cloned.1.call-done) | copy-start | bytes 7077892
  600.1 43.6 %copy-start.42 = (f32[768]{0:T(1024)S(1)}, f32[768]{0:T(1024)}, u32[]{:S(2)}) copy-start(f32[768]{0:T(1024)} %copy-done.40) | copy-start | bytes 9220
  600.1 43.6 %copy-start.46 = (f32[2,2,256]{2,1,0:T(2,128)S(1)}, f32[2,2,256]{2,1,0:T(2,128)}, u32[]{:S(2)}) copy-start(f32[2,2,256]{2,1,0:T(2,128)} %copy-done.45) | copy-start | bytes 12292
  600.1 43.6 %copy-start.49 = (f32[2,2,256]{2,1,0:T(2,128)S(1)}, f32[2,2,256]{2,1,0:T(2,128)}, u32[]{:S(2)}) copy-start(f32[2,2,256]{2,1,0:T(2,128)} %copy-done.47) | copy-start | bytes 12292
  600.2 43.6 %copy-start.53 = (f32[768]{0:T(1024)S(1)}, f32[768]{0:T(1024)}, u32[]{:S(2)}) copy-start(f32[768]{0:T(1024)} %copy-done.52) | copy-start | bytes 9220
  600.2 43.6 %copy-start.55 = (f32[2,2,256]{2,1,0:T(2,128)S(1)}, f32[2,2,256]{2,1,0:T(2,128)}, u32[]{:S(2)}) copy-start(f32[2,2,256]{2,1,0:T(2,128)} %copy-done.54) | copy-start | bytes 12292
  600.2 48.5 %copy-start.66 = (f32[2,2,256]{2,1,0:T(2,128)S(1)}, f32[2,2,256]{2,1,0:T(2,128)}, u32[]{:S(2)}) copy-start(f32[2,2,256]{2,1,0:T(2,128)} %copy-done.65) | copy-start | bytes 12292
  600.2 99.5 %all-gather.20.cloned.1.call-start = ((), (), s32[]{:S(2)}) async-start(), calls=%async_computation.17 | async-start | bytes 4718592 | tf_op jit(solution)/shard_map/all_gather | solution.py:220
  654.6 172.5 %reduce-scatter.21.cloned.1.call-start = ((), (), s32[]{:S(2)}) async-start(), calls=%async_computation.21 | async-start | bytes 5013504 | tf_op jit(solution)/shard_map/reduce_scatter | solution.py:237
  664.3 193.7 %reduce-scatter.23.cloned.1.call-start = ((), (), s32[]{:S(2)}) async-start(), calls=%async_computation.22 | async-start | bytes 5013504 | tf_op jit(solution)/shard_map/reduce_scatter | solution.py:238
  676.0 23.7 %copy-start.30 = (bf16[384,768]{0,1:T(8,128)(2,1)S(1)}, bf16[384,768]{0,1:T(8,128)(2,1)}, u32[]{:S(2)}) copy-start(bf16[384,768]{0,1:T(8,128)(2,1)} %all_gather.29) | copy-start | bytes 1769476
  676.0 243.1 %reduce-scatter.19.cloned.1.call-start = ((), (), s32[]{:S(2)}) async-start(), calls=%async_computation.20 | async-start | bytes 1253376 | tf_op jit(solution)/shard_map/reduce_scatter | solution.py:236
  712.3 278.1 %reduce-scatter.17.cloned.1.call-start = ((), (), s32[]{:S(2)}) async-start(), calls=%async_computation.19 | async-start | bytes 3760128 | tf_op jit(solution)/shard_map/reduce_scatter | solution.py:235
  723.0 12.6 %copy-start.10 = (bf16[2,512,6,64]{1,3,2,0:T(8,128)(2,1)S(1)}, bf16[2,512,6,64]{1,3,2,0:T(8,128)(2,1)}, u32[]{:S(2)}) copy-start(bf16[2,512,6,64]{1,3,2,0:T(8,128)(2,1)} %get-tuple-element.432) | copy-start | bytes 2359300 | tf_op jit(solution)/shard_map/while
  735.6 10.5 slice-start
  735.6 10.5 slice-start.1
  769.4 12.4 %copy-start.10 = (bf16[2,512,6,64]{1,3,2,0:T(8,128)(2,1)S(1)}, bf16[2,512,6,64]{1,3,2,0:T(8,128)(2,1)}, u32[]{:S(2)}) copy-start(bf16[2,512,6,64]{1,3,2,0:T(8,128)(2,1)} %get-tuple-element.432) | copy-start | bytes 2359300 | tf_op jit(solution)/shard_map/while
  781.8 10.7 slice-start
  781.8 10.7 slice-start.1
  817.0 201.2 %reduce-scatter.15.cloned.1.call-start = ((), (), s32[]{:S(2)}) async-start(), calls=%async_computation.18 | async-start | bytes 2359296 | tf_op jit(solution)/shard_map/reduce_scatter | solution.py:241
  823.6 34.4 %copy-start.21 = (f32[1536,48]{0,1:T(8,128)S(1)}, f32[1536,48]{0,1:T(8,128)}, u32[]{:S(2)}) copy-start(f32[1536,48]{0,1:T(8,128)} %param.40) | copy-start | bytes 884740
  823.7 95.5 %copy-start.29 = (f32[384,48]{0,1:T(8,128)S(1)}, f32[384,48]{0,1:T(8,128)}, u32[]{:S(2)}) copy-start(f32[384,48]{0,1:T(8,128)} %param.34) | copy-start | bytes 221188
  827.1 163.3 %copy-start.22 = (f32[48,3,384]{2,0,1:T(8,128)S(1)}, f32[48,3,384]{2,0,1:T(8,128)}, u32[]{:S(2)}) copy-start(f32[48,3,384]{2,0,1:T(8,128)} %param.31) | copy-start | bytes 663556
  829.9 239.2 %copy-start.23 = (f32[48,1536]{1,0:T(8,128)}, f32[48,1536]{1,0:T(8,128)S(1)}, u32[]{:S(2)}) copy-start(f32[48,1536]{1,0:T(8,128)S(1)} %get-tuple-element.232) | copy-start | bytes 884740
  861.2 160.0 %copy-start.71 = (f32[2,768]{1,0:T(2,128)S(1)}, f32[2,768]{1,0:T(2,128)}, u32[]{:S(2)}) copy-start(f32[2,768]{1,0:T(2,128)} %pad_maximum_fusion.1) | copy-start | bytes 18436
  861.2 202.6 %copy-start.59 = (f32[3072]{0:T(1024)S(1)}, f32[3072]{0:T(1024)}, u32[]{:S(2)}) copy-start(f32[3072]{0:T(1024)} %param.49) | copy-start | bytes 36868
  861.2 202.6 %copy-start.81 = (f32[3072]{0:T(1024)S(1)}, f32[3072]{0:T(1024)}, u32[]{:S(2)}) copy-start(f32[3072]{0:T(1024)} %param.50) | copy-start | bytes 36868
  861.2 202.6 %copy-start.82 = (f32[3072]{0:T(1024)S(1)}, f32[3072]{0:T(1024)}, u32[]{:S(2)}) copy-start(f32[3072]{0:T(1024)} %param.51) | copy-start | bytes 36868
  861.2 204.7 %copy-start.61 = (f32[2,768]{1,0:T(2,128)S(1)}, f32[2,768]{1,0:T(2,128)}, u32[]{:S(2)}) copy-start(f32[2,768]{1,0:T(2,128)} %param.43) | copy-start | bytes 18436
  861.2 204.7 %copy-start.88 = (f32[2,768]{1,0:T(2,128)S(1)}, f32[2,768]{1,0:T(2,128)}, u32[]{:S(2)}) copy-start(f32[2,768]{1,0:T(2,128)} %param.44) | copy-start | bytes 18436
  861.3 204.7 %copy-start.89 = (f32[2,768]{1,0:T(2,128)S(1)}, f32[2,768]{1,0:T(2,128)}, u32[]{:S(2)}) copy-start(f32[2,768]{1,0:T(2,128)} %param.45) | copy-start | bytes 18436
  861.3 206.1 %copy-start.44 = (f32[6,768]{1,0:T(8,128)S(1)}, f32[6,768]{1,0:T(8,128)}, u32[]{:S(2)}) copy-start(f32[6,768]{1,0:T(8,128)} %param.46) | copy-start | bytes 55300
  861.3 206.1 %copy-start.69 = (f32[6,768]{1,0:T(8,128)S(1)}, f32[6,768]{1,0:T(8,128)}, u32[]{:S(2)}) copy-start(f32[6,768]{1,0:T(8,128)} %param.47) | copy-start | bytes 55300
  861.3 206.1 %copy-start.70 = (f32[6,768]{1,0:T(8,128)S(1)}, f32[6,768]{1,0:T(8,128)}, u32[]{:S(2)}) copy-start(f32[6,768]{1,0:T(8,128)} %param.48) | copy-start | bytes 55300
  920.8 147.6 %copy-start.32 = (f32[384,48]{0,1:T(8,128)}, f32[384,48]{0,1:T(8,128)S(1)}, u32[]{:S(2)}) copy-start(f32[384,48]{0,1:T(8,128)S(1)} %get-tuple-element.234) | copy-start | bytes 221188
  920.8 147.6 %copy-start.33 = (f32[384,48]{0,1:T(8,128)}, f32[384,48]{0,1:T(8,128)S(1)}, u32[]{:S(2)}) copy-start(f32[384,48]{0,1:T(8,128)S(1)} %get-tuple-element.235) | copy-start | bytes 221188
  920.8 148.3 %copy-start.24 = (f32[48,1536]{1,0:T(8,128)S(1)}, f32[48,1536]{1,0:T(8,128)}, u32[]{:S(2)}) copy-start(f32[48,1536]{1,0:T(8,128)} %get-tuple-element.233) | copy-start | bytes 884740
  991.9 78.1 %copy-start.27 = (f32[48,3,384]{2,0,1:T(8,128)}, f32[48,3,384]{2,0,1:T(8,128)S(1)}, u32[]{:S(2)}) copy-start(f32[48,3,384]{2,0,1:T(8,128)S(1)} %get-tuple-element.236) | copy-start | bytes 663556
  991.9 78.1 %copy-start.28 = (f32[48,3,384]{2,0,1:T(8,128)}, f32[48,3,384]{2,0,1:T(8,128)S(1)}, u32[]{:S(2)}) copy-start(f32[48,3,384]{2,0,1:T(8,128)S(1)} %get-tuple-element.237) | copy-start | bytes 663556
  1018.2 51.8 %copy-start.25 = (f32[1536,48]{0,1:T(8,128)S(1)}, f32[1536,48]{0,1:T(8,128)}, u32[]{:S(2)}) copy-start(f32[1536,48]{0,1:T(8,128)} %get-tuple-element.230) | copy-start | bytes 884740
  1018.2 51.8 %copy-start.26 = (f32[1536,48]{0,1:T(8,128)S(1)}, f32[1536,48]{0,1:T(8,128)}, u32[]{:S(2)}) copy-start(f32[1536,48]{0,1:T(8,128)} %get-tuple-element.231) | copy-start | bytes 884740
  (71 other events, 268.1 us)
Sparse Core Ops, SparseCore 0:
  10.9 44.3 all-gather.9
  56.8 26.1 all-gather.7
  202.5 43.3 reduce-scatter.8
  248.8 42.2 all-gather.13
  292.5 43.6 all-gather.11
  339.3 42.2 all-gather.15
  390.8 42.1 reduce-scatter.10
  535.2 40.7 all-gather.17
  600.3 43.3 reduce-scatter.12
  654.7 44.9 all-gather.19
  704.1 75.5 reduce-scatter.20
  783.4 74.5 reduce-scatter.22
  862.1 57.0 reduce-scatter.18
  923.4 67.0 reduce-scatter.16
  993.2 24.9 reduce-scatter.14
where the time goes:
time: 1090 us; the launch traced here: 1080 us
  waiting for transfers between devices  474 us (43%)
  matrix products  190 us (17%)
  local copies, waits for them, and re-layouts  159 us (15%)
  blocking collectives  141 us (13%)
  other arithmetic  84 us (8%)
  between operations  20.7 us (2%)
  starting transfers between devices  11.5 us (1%)
    all_gather x1, blocking collectives, shards(): lax.all_gather(pooled_part, ('dp', 'tensor'), axis=1, tiled=True)  74 us
    reduce_scatter x1, waiting for transfers between devices, shards(): lax.psum_scatter(grad_attn_weight, 'dp', scatter_dimension=0, tiled=True)  69.6 us
    dot_general x8, matrix products, contract(): lax.dot_general(left_side, right_side, (((left_dim,), (right_dim,)), ((),...  58.3 us
    reduce_scatter x1, waiting for transfers between devices, shards(): lax.psum_scatter(grad_out, 'dp', scatter_dimension=1, tiled=True)  56.9 us
    while x62, local copies, waits for them, and re-layouts  47.6 us
    all_gather x1, waiting for transfers between devices, shards(): lax.all_gather(normed.astype(jnp.bfloat16), 'tensor', axis=2, tiled=True)  45.2 us
    reduce_scatter x1, waiting for transfers between devices, shards(): lax.psum_scatter(normed_back.astype(jnp.bfloat16), 'tensor', scatter_dime...  43.4 us
    all_gather x1, waiting for transfers between devices, shards(): grad_ffn_full = lax.all_gather(grad_ffn, 'tensor', axis=2, tiled=True)  40.5 us
  transfers between devices with their start and end apart: 15, of which 14 were waited for; matrix products, arithmetic and copies ran while one was open for 20% of the time, Pallas kernels for 0%

commit v1 on v0

--- a/solution.py
+++ b/solution.py
@@ -295,7 +295,7 @@
         ]
     )
     summed_squares, gain_total, shift_total, hidden_total = lax.psum(
-        (squares, gain_grads, shift_grads, hidden_grads), ("dp", "tensor")
+        lax.psum((squares, gain_grads, shift_grads, hidden_grads), "tensor"), "dp"
     )
     trust_ratio = jnp.sqrt(summed_squares[:6]) / jnp.sqrt(summed_squares[6:])
     new_attn = attn_weight - 0.25 * trust_ratio[0:3][None, :, None] * attn_update

time: 1090 us -> 1120 us (1.028)
  blocking collectives: 141 us -> 168 us
    psum x1 -> x2, blocking collectives: 40.1 us -> 67 us  [the longest x1 59.6 us: shards(): lax.psum(lax.psum((squares, gain_grads, shift_grads, hidden_grads), 'tens...]
where the time goes in v1:
time: 1120 us; the launch traced here: 1110 us
  waiting for transfers between devices  474 us (42%)
  matrix products  190 us (17%)
  blocking collectives  168 us (15%)
  local copies, waits for them, and re-layouts  159 us (14%)
  other arithmetic  84 us (8%)
  between operations  20.7 us (2%)
  starting transfers between devices  11.5 us (1%)
    all_gather x1, blocking collectives, shards(): lax.all_gather(pooled_part, ('dp', 'tensor'), axis=1, tiled=True)  74.1 us
    reduce_scatter x1, waiting for transfers between devices, shards(): lax.psum_scatter(grad_attn_weight, 'dp', scatter_dimension=0, tiled=True)  69.6 us
    psum x1, blocking collectives, shards(): lax.psum(lax.psum((squares, gain_grads, shift_grads, hidden_grads), 'tens...  59.6 us
    dot_general x8, matrix products, contract(): lax.dot_general(left_side, right_side, (((left_dim,), (right_dim,)), ((),...  58.3 us
    reduce_scatter x1, waiting for transfers between devices, shards(): lax.psum_scatter(grad_out, 'dp', scatter_dimension=1, tiled=True)  56.9 us
    while x62, local copies, waits for them, and re-layouts  47.6 us
    all_gather x1, waiting for transfers between devices, shards(): lax.all_gather(normed.astype(jnp.bfloat16), 'tensor', axis=2, tiled=True)  45.2 us
    reduce_scatter x1, waiting for transfers between devices, shards(): lax.psum_scatter(normed_back.astype(jnp.bfloat16), 'tensor', scatter_dime...  43.4 us
  transfers between devices with their start and end apart: 15, of which 14 were waited for; matrix products, arithmetic and copies ran while one was open for 20% of the time, Pallas kernels for 0%

profile of v1, /device:TPU:0, one launch (start us, length us, event | category | flops | bytes accessed | tf_op | source)
XLA Modules:
  0.0 1107.4 jit_solution(13222384462289387249)
XLA Ops:
  14.4 27.1 %all_gather.29 = bf16[384,768]{0,1:T(8,128)(2,1)} all-gather(bf16[384,48]{0,1:T(8,128)(2,1)S(1)} %convert_element_type.122), channel_id=1, replica_groups=mesh['dp'=16,'tensor'=2] {'dp'}, dimensions={1}, use_global_device_ids=true | all-gather | bytes 626688 | tf_op jit(solution)/shard_map/all_gather | solution.py:139
  41.6 13.7 %all-gather.10.cloned.1.call-done = bf16[768,3,384]{2,0,1:T(8,128)(2,1)} async-done(((bf16[48,3,384]{2,0,1:T(8,128)(2,1)}), bf16[768,3,384]{2,0,1:T(8,128)(2,1)}) %all-gather.10.cloned.1.call-update) | async-done | bytes 1769488 | tf_op jit(solution)/shard_map/all_gather | solution.py:138
  55.3 3.9 copy.163
  59.1 23.8 %all-gather.8.cloned.1.call-done = bf16[2,512,768]{2,1,0:T(8,128)(2,1)} async-done(((bf16[2,256,768]{2,1,0:T(8,128)(2,1)}), bf16[2,512,768]{2,1,0:T(8,128)(2,1)}) %all-gather.8.cloned.1.call-update) | async-done | bytes 1572880 | tf_op jit(solution)/shard_map/all_gather | solution.py:143
  83.0 4.0 add_convert_fusion.1
  88.1 108.0 %while.22 = (s32[]{:T(128)}, bf16[2,2,512,384]{2,3,1,0:T(8,128)(2,1)}, f32[2,6,512]{2,1,0:T(8,128)}, bf16[2,512,6,64]{1,3,2,0:T(8,128)(2,1)}, s32[2,2,6,512,40]{...) while((s32[]{:T(128)}, ...), condition=%wide.region_3.4_spmd, body=%wide.region_0.3_spmd.sunk | while | flops 632681472 | bytes 140713456 | solution.py:161
  88.4 3.6 shift_right_arithmetic.162
  92.0 6.3 slice.162
  98.3 19.1 %copy.239 = s32[2,6,512,512]{3,2,1,0:T(8,128)} copy(s32[2,6,512,512]{2,0,3,1:T(2,128)} %slice.162) | data formatting | bytes 25165824 | tf_op jit(solution)/shard_map/while
  121.6 3.7 exponential_multiply_fusion.2
  125.3 6.6 copy.240
  131.9 8.9 fusion.134
  142.4 3.6 shift_right_arithmetic.162
  146.0 6.3 slice.162
  152.3 19.1 %copy.239 = s32[2,6,512,512]{3,2,1,0:T(8,128)} copy(s32[2,6,512,512]{2,0,3,1:T(2,128)} %slice.162) | data formatting | bytes 25165824 | tf_op jit(solution)/shard_map/while
  175.6 3.7 exponential_multiply_fusion.2
  179.3 6.6 copy.240
  185.9 8.9 fusion.134
  196.1 6.3 convolution_convert_fusion.3
  204.2 9.9 all-gather.12.cloned.1.call-start
  220.5 4.1 copy.202
  224.7 21.3 %reduce-scatter.9.cloned.1.call-done = bf16[2,2,256,768]{3,2,1,0:T(8,128)(2,1)} async-done(((bf16[2,2,512,768]{3,2,1,0:T(8,128)(2,1)}), bf16[2,2,256,768]{3,2,1,0:T(8,128)(2,1)}) %reduce-scatter.9.cloned.1.call-update) | async-done | bytes 1572880 | tf_op jit(solution)/shard_map/reduce_scatter | solution.py:170
  253.2 37.9 %all-gather.14.cloned.1.call-done = bf16[768,1536]{1,0:T(8,128)(2,1)} async-done(((bf16[48,1536]{1,0:T(8,128)(2,1)}), bf16[768,1536]{1,0:T(8,128)(2,1)}) %all-gather.14.cloned.1.call-update) | async-done | bytes 2359312 | tf_op jit(solution)/shard_map/all_gather | solution.py:140
  291.1 45.2 %all-gather.12.cloned.1.call-done = bf16[2,2,512,768]{3,2,1,0:T(8,128)(2,1)} async-done(((bf16[2,2,256,768]{3,2,1,0:T(8,128)(2,1)}), bf16[2,2,512,768]{3,2,1,0:T(8,128)(2,1)}) %all-gather.12.cloned.1.call-update) | async-done | bytes 3145744 | tf_op jit(solution)/shard_map/all_gather | solution.py:179
  336.3 34.9 %multiply_convert_fusion.6 = (bf16[2048,1536]{1,0:T(8,128)(2,1)}, f32[2048,1536]{1,0:T(8,128)}, f32[2048,1536]{1,0:T(8,128)}) fusion(f32[1536]{0:T(1024)S(1)} %dynamic_slice.48, bf16[2048,768]{1,0:T(8,128)(2,1)} %bitcast.269, bf16[768,1536]{1,0:T(8,128)(2,1)} %all-gather.14.cloned.1.call-done), kind=kOutput, calls=%fused_computation.68 | convolution fusion | flops 5039456256 | bytes 36968448 | tf_op jit(solution)/shard_map/dot_general | solution.py:182
  371.2 10.3 all-gather.16.cloned.1.call-done
  381.6 9.1 convolution_convert_fusion.1
  392.9 3.6 copy.203
  397.0 36.0 %reduce-scatter.11.cloned.1.call-done = bf16[2,2,256,768]{3,2,1,0:T(8,128)(2,1)} async-done(((bf16[2,2,512,768]{3,2,1,0:T(8,128)(2,1)}), bf16[2,2,256,768]{3,2,1,0:T(8,128)(2,1)}) %reduce-scatter.11.cloned.1.call-update) | async-done | bytes 1572880 | tf_op jit(solution)/shard_map/reduce_scatter | solution.py:189
  433.0 4.1 fusion.84
  438.9 74.1 %all_gather.33 = f32[2,64,768]{2,0,1:T(2,128)} all-gather(f32[2,2,768]{2,0,1:T(2,128)S(1)} %copy.168), channel_id=1, replica_groups=mesh['dp'=16,'tensor'=2] {'dp','tensor'}, dimensions={1}, use_global_device_ids=true | all-gather | bytes 405504 | tf_op jit(solution)/shard_map/all_gather | solution.py:196
  535.6 40.5 %all-gather.18.cloned.1.call-done = bf16[2,2,512,768]{3,2,1,0:T(8,128)(2,1)} async-done(((bf16[2,2,256,768]{3,2,1,0:T(8,128)(2,1)}), bf16[2,2,512,768]{3,2,1,0:T(8,128)(2,1)}) %all-gather.18.cloned.1.call-update) | async-done | bytes 3145744 | tf_op jit(solution)/shard_map/all_gather | solution.py:208
  576.1 17.6 %convert_reduce_fusion = (f32[1536]{0:T(1024)}, bf16[2048,1536]{1,0:T(8,128)(2,1)S(1)}) fusion(f32[2048,1536]{1,0:T(8,128)} %get-tuple-element.247, bf16[2048,768]{1,0:T(8,128)(2,1)} %bitcast.271, bf16[1536,768]{0,1:T(8,128)(2,1)} %all-gather.16.cloned.1.call-done, f32[2048,1536]{1,0:T(8,128)} %get-tuple-element.274, f32[1536]{0:T(1024)S(1)} %copy-done.87), kind=kOutput, calls=%fused_computation.66 | convolution fusion | flops 4885314048 | bytes 36974592 | tf_op jit(solution)/shard_map/dot_general | solution.py:35
  593.7 6.5 convolution_convert_fusion
  600.3 43.4 %reduce-scatter.13.cloned.1.call-done = bf16[2,2,256,768]{3,2,1,0:T(8,128)(2,1)} async-done(((bf16[2,2,512,768]{3,2,1,0:T(8,128)(2,1)}), bf16[2,2,256,768]{3,2,1,0:T(8,128)(2,1)}) %reduce-scatter.13.cloned.1.call-update) | async-done | bytes 1572880 | tf_op jit(solution)/shard_map/reduce_scatter | solution.py:215
  643.8 5.0 multiply_reduce_fusion.3
  654.7 9.6 fusion.92
  666.5 9.5 fusion.93
  676.1 23.7 %all-gather.20.cloned.1.call-done = bf16[2,2,512,768]{3,2,1,0:T(8,128)(2,1)} async-done(((bf16[2,2,256,768]{3,2,1,0:T(8,128)(2,1)}), bf16[2,2,512,768]{3,2,1,0:T(8,128)(2,1)}) %all-gather.20.cloned.1.call-update) | async-done | bytes 3145744 | tf_op jit(solution)/shard_map/all_gather | solution.py:220
  699.8 3.7 convolution_convert_fusion.2
  707.9 4.5 convolution_bitcast_fusion
  712.7 93.9 %while.23 = (s32[]{:T(128)}, bf16[2,512,3,6,64]{1,4,3,2,0:T(8,128)(2,1)}, bf16[2,512,6,64]{1,3,2,0:T(8,128)(2,1)S(1)}, bf16[2,512,6,64]{1,3,2,0:T(8,128)(2,1)}, ...) while((s32[]{:T(128)}, ...), condition=%wide.region_26.27_spmd, body=%wide.region_23.26_spmd.sunk | while | flops 1462367232 | bytes 228946432 | solution.py:228
  713.0 3.6 shift_right_arithmetic.169
  716.6 6.3 slice.164
  723.1 12.5 %fusion.142 = f32[6,512,512]{1,2,0:T(8,128)} fusion(s32[2,6,512,512]{2,0,3,1:T(2,128)} %slice.164, s32[512]{0:T(512)S(1)} %slice.165, bf16[2,2,512,6,64]{2,4,1,3,0:T(8,128)(2,1)} %get-tuple-element.439, s32[]{:T(128)S(6)} %copy.259, bf16[2,512,6,64]{1,3,2,0:T(8,128)(2,1)} %get-tuple-element.438), kind=kOutput, calls=%fused_computation.27.clone.1 | convolution fusion | flops 419954688 | bytes 20057088 | tf_op jit(solution)/shard_map/while/body/eval_jaxpr/vqhd,khd->vhqk/dot_general | solution.py:68
  735.7 4.8 multiply_reduce_fusion.25
  740.5 5.6 multiply_convert_fusion.18
  747.4 6.1 fusion.143
  759.5 3.6 shift_right_arithmetic.169
  763.1 6.3 slice.164
  769.5 12.4 %fusion.142 = f32[6,512,512]{1,2,0:T(8,128)} fusion(s32[2,6,512,512]{2,0,3,1:T(2,128)} %slice.164, s32[512]{0:T(512)S(1)} %slice.165, bf16[2,2,512,6,64]{2,4,1,3,0:T(8,128)(2,1)} %get-tuple-element.439, s32[]{:T(128)S(6)} %copy.259, bf16[2,512,6,64]{1,3,2,0:T(8,128)(2,1)} %get-tuple-element.438), kind=kOutput, calls=%fused_computation.27.clone.1 | convolution fusion | flops 419954688 | bytes 20057088 | tf_op jit(solution)/shard_map/while/body/eval_jaxpr/vqhd,khd->vhqk/dot_general | solution.py:68
  782.0 4.8 multiply_reduce_fusion.25
  786.8 5.9 multiply_convert_fusion.18
  794.1 6.3 fusion.143
  800.5 3.4 fusion.144
  806.6 4.1 copy.178
  818.8 5.0 convolution_convert_fusion.4
  830.0 28.1 %reduce-scatter.23.cloned.1.call-done = f32[1536,48]{0,1:T(8,128)} async-done(((f32[1536,768]{0,1:T(8,128)}), f32[1536,48]{0,1:T(8,128)}) %reduce-scatter.23.cloned.1.call-update) | async-done | bytes 294928 | tf_op jit(solution)/shard_map/reduce_scatter | solution.py:238
  862.3 56.9 %reduce-scatter.19.cloned.1.call-done = f32[384,48]{0,1:T(8,128)} async-done(((f32[384,768]{0,1:T(8,128)}), f32[384,48]{0,1:T(8,128)}) %reduce-scatter.19.cloned.1.call-update) | async-done | bytes 73744 | tf_op jit(solution)/shard_map/reduce_scatter | solution.py:236
  920.9 69.6 %reduce-scatter.17.cloned.1.call-done = f32[48,3,384]{2,0,1:T(8,128)} async-done(((f32[768,3,384]{2,0,1:T(8,128)}), f32[48,3,384]{2,0,1:T(8,128)}) %reduce-scatter.17.cloned.1.call-update) | async-done | bytes 221200 | tf_op jit(solution)/shard_map/reduce_scatter | solution.py:235
  992.0 4.0 concatenate.8
  995.9 22.4 %reduce-scatter.15.cloned.1.call-done = bf16[2,256,768]{2,1,0:T(8,128)(2,1)} async-done(((bf16[2,512,768]{2,1,0:T(8,128)(2,1)}), bf16[2,256,768]{2,1,0:T(8,128)(2,1)}) %reduce-scatter.15.cloned.1.call-update) | async-done | bytes 786448 | tf_op jit(solution)/shard_map/reduce_scatter | solution.py:241
  1021.3 7.4 all-reduce.3
  1028.7 59.6 %all-reduce.2 = (f32[12]{0:T(128)S(1)}, f32[2,768]{1,0:T(2,128)S(1)}, f32[6,768]{1,0:T(8,128)S(1)}, f32[3072]{0:T(1024)S(1)}) all-reduce(f32[12]{0:T(128)S(1)} %get-tuple-element.216, f32[2,768]{1,0:T(2,128)S(1)} %get-tuple-element.217, f32[6,768]{1,0:T(8,128)S(1)} %get-tuple-element.218, ...), channel_id=1, replica_groups=mesh['dp'=16,'tensor'=2] {'dp'}, use_global_device_ids=true, to_apply=%region_42.43 | all-reduce | flops 9228 | bytes 73824 | tf_op jit(solution)/shard_map/psum | solution.py:297
  (416 shorter events, 117.7 us)
Async XLA Ops:
  7.2 48.1 %all-gather.10.cloned.1.call-start = ((), (), s32[]{:S(2)}) async-start(), calls=%async_computation.9 | async-start | bytes 1880064 | tf_op jit(solution)/shard_map/all_gather | solution.py:138
  8.9 74.1 %all-gather.8.cloned.1.call-start = ((), (), s32[]{:S(2)}) async-start(), calls=%async_computation.8 | async-start | bytes 2359296 | tf_op jit(solution)/shard_map/all_gather | solution.py:143
  9.6 236.3 %reduce-scatter.9.cloned.1.call-start = ((), (), s32[]{:S(2)}) async-start(), calls=%async_computation.10 | async-start | bytes 4718592 | tf_op jit(solution)/shard_map/reduce_scatter | solution.py:170
  131.9 9.0 copy-start.97
  185.9 9.0 copy-start.97
  202.4 88.7 %all-gather.14.cloned.1.call-start = ((), (), s32[]{:S(2)}) async-start(), calls=%async_computation.12 | async-start | bytes 2506752 | tf_op jit(solution)/shard_map/all_gather | solution.py:140
  202.5 14.2 %copy-start.31 = (s32[2,2,2,256,52]{3,2,4,1,0:T(2,128)S(1)}, s32[2,2,2,256,52]{3,2,4,1,0:T(2,128)}, u32[]{:S(2)}) copy-start(s32[2,2,2,256,52]{3,2,4,1,0:T(2,128)} %param.30) | copy-start | bytes 1277956
  204.2 132.1 %all-gather.12.cloned.1.call-start = ((), (), s32[]{:S(2)}) async-start(), calls=%async_computation.11 | async-start | bytes 4718592 | tf_op jit(solution)/shard_map/all_gather | solution.py:179
  216.7 216.2 %copy-start.50 = (s32[780]{0:T(1024)}, s32[780]{0:T(1024)S(1)}, u32[]{:S(2)}) copy-start(s32[780]{0:T(1024)S(1)} %shift_right_arithmetic.92) | copy-start | bytes 9364
  220.5 25.4 %copy-start.72 = (f32[768]{0:T(1024)S(1)}, f32[768]{0:T(1024)}, u32[]{:S(2)}) copy-start(f32[768]{0:T(1024)} %get-tuple-element.176) | copy-start | bytes 9220
  224.6 24.2 %copy-start.12 = (s32[2,2,256,768]{3,2,1,0:T(8,128)}, s32[2,2,256,768]{3,2,1,0:T(8,128)S(1)}, u32[]{:S(2)}) copy-start(s32[2,2,256,768]{3,2,1,0:T(8,128)S(1)} %copy.202) | copy-start | bytes 9437188
  224.6 208.3 %copy-start.52 = (f32[768]{0:T(1024)}, f32[768]{0:T(1024)S(1)}, u32[]{:S(2)}) copy-start(f32[768]{0:T(1024)S(1)} %get-tuple-element.181) | copy-start | bytes 9220
  224.7 213.6 %copy-start.40 = (f32[768]{0:T(1024)}, f32[768]{0:T(1024)S(1)}, u32[]{:S(2)}) copy-start(f32[768]{0:T(1024)S(1)} %get-tuple-element.180) | copy-start | bytes 9220
  248.9 184.1 %copy-start.45 = (f32[2,2,256]{2,1,0:T(2,128)}, f32[2,2,256]{2,1,0:T(2,128)S(1)}, u32[]{:S(2)}) copy-start(f32[2,2,256]{2,1,0:T(2,128)S(1)} %broadcast_multiply_fusion.3) | copy-start | bytes 12292
  249.4 183.5 %copy-start.54 = (f32[2,2,256]{2,1,0:T(2,128)}, f32[2,2,256]{2,1,0:T(2,128)S(1)}, u32[]{:S(2)}) copy-start(f32[2,2,256]{2,1,0:T(2,128)S(1)} %fusion.71) | copy-start | bytes 12292
  252.3 129.3 %all-gather.16.cloned.1.call-start = ((), (), s32[]{:S(2)}) async-start(), calls=%async_computation.13 | async-start | bytes 2506752 | tf_op jit(solution)/shard_map/all_gather | solution.py:141
  253.1 179.9 %reduce-scatter.11.cloned.1.call-start = ((), (), s32[]{:S(2)}) async-start(), calls=%async_computation.14 | async-start | bytes 4718592 | tf_op jit(solution)/shard_map/reduce_scatter | solution.py:189
  253.2 118.0 %copy-start.86 = (f32[1536]{0:T(1024)}, f32[1536]{0:T(1024)S(1)}, u32[]{:S(2)}) copy-start(f32[1536]{0:T(1024)S(1)} %dynamic_slice.48) | copy-start | bytes 18436
  390.7 185.4 %all-gather.18.cloned.1.call-start = ((), (), s32[]{:S(2)}) async-start(), calls=%async_computation.15 | async-start | bytes 4718592 | tf_op jit(solution)/shard_map/all_gather | solution.py:208
  392.9 40.1 %copy-start.75 = (f32[768]{0:T(1024)S(1)}, f32[768]{0:T(1024)}, u32[]{:S(2)}) copy-start(f32[768]{0:T(1024)} %get-tuple-element.174) | copy-start | bytes 9220
  437.7 77.1 %copy-start.47 = (f32[2,2,256]{2,1,0:T(2,128)}, f32[2,2,256]{2,1,0:T(2,128)S(1)}, u32[]{:S(2)}) copy-start(f32[2,2,256]{2,1,0:T(2,128)S(1)} %fusion.72) | copy-start | bytes 12292
  532.1 44.0 %copy-start.87 = (f32[1536]{0:T(1024)S(1)}, f32[1536]{0:T(1024)}, u32[]{:S(2)}) copy-start(f32[1536]{0:T(1024)} %copy-done.86) | copy-start | bytes 18436
  535.1 108.6 %reduce-scatter.13.cloned.1.call-start = ((), (), s32[]{:S(2)}) async-start(), calls=%async_computation.16 | async-start | bytes 4718592 | tf_op jit(solution)/shard_map/reduce_scatter | solution.py:215
  576.1 17.6 %copy-start.95 = (bf16[768,1536]{1,0:T(8,128)(2,1)S(1)}, bf16[768,1536]{1,0:T(8,128)(2,1)}, u32[]{:S(2)}) copy-start(bf16[768,1536]{1,0:T(8,128)(2,1)} %all-gather.14.cloned.1.call-done) | copy-start | bytes 7077892
  600.2 43.6 %copy-start.42 = (f32[768]{0:T(1024)S(1)}, f32[768]{0:T(1024)}, u32[]{:S(2)}) copy-start(f32[768]{0:T(1024)} %copy-done.40) | copy-start | bytes 9220
  600.2 43.6 %copy-start.46 = (f32[2,2,256]{2,1,0:T(2,128)S(1)}, f32[2,2,256]{2,1,0:T(2,128)}, u32[]{:S(2)}) copy-start(f32[2,2,256]{2,1,0:T(2,128)} %copy-done.45) | copy-start | bytes 12292
  600.2 43.6 %copy-start.49 = (f32[2,2,256]{2,1,0:T(2,128)S(1)}, f32[2,2,256]{2,1,0:T(2,128)}, u32[]{:S(2)}) copy-start(f32[2,2,256]{2,1,0:T(2,128)} %copy-done.47) | copy-start | bytes 12292
  600.2 43.6 %copy-start.53 = (f32[768]{0:T(1024)S(1)}, f32[768]{0:T(1024)}, u32[]{:S(2)}) copy-start(f32[768]{0:T(1024)} %copy-done.52) | copy-start | bytes 9220
  600.2 43.6 %copy-start.55 = (f32[2,2,256]{2,1,0:T(2,128)S(1)}, f32[2,2,256]{2,1,0:T(2,128)}, u32[]{:S(2)}) copy-start(f32[2,2,256]{2,1,0:T(2,128)} %copy-done.54) | copy-start | bytes 12292
  600.2 48.5 %copy-start.66 = (f32[2,2,256]{2,1,0:T(2,128)S(1)}, f32[2,2,256]{2,1,0:T(2,128)}, u32[]{:S(2)}) copy-start(f32[2,2,256]{2,1,0:T(2,128)} %copy-done.65) | copy-start | bytes 12292
  600.3 99.5 %all-gather.20.cloned.1.call-start = ((), (), s32[]{:S(2)}) async-start(), calls=%async_computation.17 | async-start | bytes 4718592 | tf_op jit(solution)/shard_map/all_gather | solution.py:220
  654.7 172.6 %reduce-scatter.21.cloned.1.call-start = ((), (), s32[]{:S(2)}) async-start(), calls=%async_computation.21 | async-start | bytes 5013504 | tf_op jit(solution)/shard_map/reduce_scatter | solution.py:237
  664.3 193.8 %reduce-scatter.23.cloned.1.call-start = ((), (), s32[]{:S(2)}) async-start(), calls=%async_computation.22 | async-start | bytes 5013504 | tf_op jit(solution)/shard_map/reduce_scatter | solution.py:238
  676.0 23.8 %copy-start.30 = (bf16[384,768]{0,1:T(8,128)(2,1)S(1)}, bf16[384,768]{0,1:T(8,128)(2,1)}, u32[]{:S(2)}) copy-start(bf16[384,768]{0,1:T(8,128)(2,1)} %all_gather.29) | copy-start | bytes 1769476
  676.0 243.2 %reduce-scatter.19.cloned.1.call-start = ((), (), s32[]{:S(2)}) async-start(), calls=%async_computation.20 | async-start | bytes 1253376 | tf_op jit(solution)/shard_map/reduce_scatter | solution.py:236
  712.4 278.1 %reduce-scatter.17.cloned.1.call-start = ((), (), s32[]{:S(2)}) async-start(), calls=%async_computation.19 | async-start | bytes 3760128 | tf_op jit(solution)/shard_map/reduce_scatter | solution.py:235
  723.1 12.5 %copy-start.10 = (bf16[2,512,6,64]{1,3,2,0:T(8,128)(2,1)S(1)}, bf16[2,512,6,64]{1,3,2,0:T(8,128)(2,1)}, u32[]{:S(2)}) copy-start(bf16[2,512,6,64]{1,3,2,0:T(8,128)(2,1)} %get-tuple-element.436) | copy-start | bytes 2359300 | tf_op jit(solution)/shard_map/while
  735.6 10.5 slice-start
  735.6 10.5 slice-start.1
  769.5 12.4 %copy-start.10 = (bf16[2,512,6,64]{1,3,2,0:T(8,128)(2,1)S(1)}, bf16[2,512,6,64]{1,3,2,0:T(8,128)(2,1)}, u32[]{:S(2)}) copy-start(bf16[2,512,6,64]{1,3,2,0:T(8,128)(2,1)} %get-tuple-element.436) | copy-start | bytes 2359300 | tf_op jit(solution)/shard_map/while
  781.9 10.7 slice-start
  781.9 10.7 slice-start.1
  817.1 201.2 %reduce-scatter.15.cloned.1.call-start = ((), (), s32[]{:S(2)}) async-start(), calls=%async_computation.18 | async-start | bytes 2359296 | tf_op jit(solution)/shard_map/reduce_scatter | solution.py:241
  823.8 34.3 %copy-start.21 = (f32[1536,48]{0,1:T(8,128)S(1)}, f32[1536,48]{0,1:T(8,128)}, u32[]{:S(2)}) copy-start(f32[1536,48]{0,1:T(8,128)} %param.40) | copy-start | bytes 884740
  823.8 95.4 %copy-start.29 = (f32[384,48]{0,1:T(8,128)S(1)}, f32[384,48]{0,1:T(8,128)}, u32[]{:S(2)}) copy-start(f32[384,48]{0,1:T(8,128)} %param.34) | copy-start | bytes 221188
  827.3 163.2 %copy-start.22 = (f32[48,3,384]{2,0,1:T(8,128)S(1)}, f32[48,3,384]{2,0,1:T(8,128)}, u32[]{:S(2)}) copy-start(f32[48,3,384]{2,0,1:T(8,128)} %param.31) | copy-start | bytes 663556
  830.0 266.1 %copy-start.23 = (f32[48,1536]{1,0:T(8,128)}, f32[48,1536]{1,0:T(8,128)S(1)}, u32[]{:S(2)}) copy-start(f32[48,1536]{1,0:T(8,128)S(1)} %get-tuple-element.236) | copy-start | bytes 884740
  861.3 160.0 %copy-start.71 = (f32[2,768]{1,0:T(2,128)S(1)}, f32[2,768]{1,0:T(2,128)}, u32[]{:S(2)}) copy-start(f32[2,768]{1,0:T(2,128)} %pad_maximum_fusion.1) | copy-start | bytes 18436
  861.3 229.6 %copy-start.59 = (f32[3072]{0:T(1024)S(1)}, f32[3072]{0:T(1024)}, u32[]{:S(2)}) copy-start(f32[3072]{0:T(1024)} %param.49) | copy-start | bytes 36868
  861.3 229.6 %copy-start.81 = (f32[3072]{0:T(1024)S(1)}, f32[3072]{0:T(1024)}, u32[]{:S(2)}) copy-start(f32[3072]{0:T(1024)} %param.50) | copy-start | bytes 36868
  861.3 229.6 %copy-start.82 = (f32[3072]{0:T(1024)S(1)}, f32[3072]{0:T(1024)}, u32[]{:S(2)}) copy-start(f32[3072]{0:T(1024)} %param.51) | copy-start | bytes 36868
  861.3 231.7 %copy-start.61 = (f32[2,768]{1,0:T(2,128)S(1)}, f32[2,768]{1,0:T(2,128)}, u32[]{:S(2)}) copy-start(f32[2,768]{1,0:T(2,128)} %param.43) | copy-start | bytes 18436
  861.3 231.7 %copy-start.88 = (f32[2,768]{1,0:T(2,128)S(1)}, f32[2,768]{1,0:T(2,128)}, u32[]{:S(2)}) copy-start(f32[2,768]{1,0:T(2,128)} %param.44) | copy-start | bytes 18436
  861.3 231.7 %copy-start.89 = (f32[2,768]{1,0:T(2,128)S(1)}, f32[2,768]{1,0:T(2,128)}, u32[]{:S(2)}) copy-start(f32[2,768]{1,0:T(2,128)} %param.45) | copy-start | bytes 18436
  861.3 233.1 %copy-start.44 = (f32[6,768]{1,0:T(8,128)S(1)}, f32[6,768]{1,0:T(8,128)}, u32[]{:S(2)}) copy-start(f32[6,768]{1,0:T(8,128)} %param.46) | copy-start | bytes 55300
  861.4 233.1 %copy-start.69 = (f32[6,768]{1,0:T(8,128)S(1)}, f32[6,768]{1,0:T(8,128)}, u32[]{:S(2)}) copy-start(f32[6,768]{1,0:T(8,128)} %param.47) | copy-start | bytes 55300
  861.4 233.1 %copy-start.70 = (f32[6,768]{1,0:T(8,128)S(1)}, f32[6,768]{1,0:T(8,128)}, u32[]{:S(2)}) copy-start(f32[6,768]{1,0:T(8,128)} %param.48) | copy-start | bytes 55300
  920.9 174.6 %copy-start.32 = (f32[384,48]{0,1:T(8,128)}, f32[384,48]{0,1:T(8,128)S(1)}, u32[]{:S(2)}) copy-start(f32[384,48]{0,1:T(8,128)S(1)} %get-tuple-element.238) | copy-start | bytes 221188
  920.9 174.6 %copy-start.33 = (f32[384,48]{0,1:T(8,128)}, f32[384,48]{0,1:T(8,128)S(1)}, u32[]{:S(2)}) copy-start(f32[384,48]{0,1:T(8,128)S(1)} %get-tuple-element.239) | copy-start | bytes 221188
  920.9 175.3 %copy-start.24 = (f32[48,1536]{1,0:T(8,128)S(1)}, f32[48,1536]{1,0:T(8,128)}, u32[]{:S(2)}) copy-start(f32[48,1536]{1,0:T(8,128)} %get-tuple-element.237) | copy-start | bytes 884740
  992.0 105.1 %copy-start.27 = (f32[48,3,384]{2,0,1:T(8,128)}, f32[48,3,384]{2,0,1:T(8,128)S(1)}, u32[]{:S(2)}) copy-start(f32[48,3,384]{2,0,1:T(8,128)S(1)} %get-tuple-element.240) | copy-start | bytes 663556
  992.0 105.1 %copy-start.28 = (f32[48,3,384]{2,0,1:T(8,128)}, f32[48,3,384]{2,0,1:T(8,128)S(1)}, u32[]{:S(2)}) copy-start(f32[48,3,384]{2,0,1:T(8,128)S(1)} %get-tuple-element.241) | copy-start | bytes 663556
  1018.3 78.7 %copy-start.25 = (f32[1536,48]{0,1:T(8,128)S(1)}, f32[1536,48]{0,1:T(8,128)}, u32[]{:S(2)}) copy-start(f32[1536,48]{0,1:T(8,128)} %get-tuple-element.234) | copy-start | bytes 884740
  1018.3 78.7 %copy-start.26 = (f32[1536,48]{0,1:T(8,128)S(1)}, f32[1536,48]{0,1:T(8,128)}, u32[]{:S(2)}) copy-start(f32[1536,48]{0,1:T(8,128)} %get-tuple-element.235) | copy-start | bytes 884740
  (71 other events, 268.1 us)
Sparse Core Ops, SparseCore 0:
  10.9 44.3 all-gather.9
  56.8 26.1 all-gather.7
  202.5 43.3 reduce-scatter.8
  248.9 42.2 all-gather.13
  292.6 43.6 all-gather.11
  339.3 42.2 all-gather.15
  390.8 42.0 reduce-scatter.10
  535.3 40.7 all-gather.17
  600.4 43.3 reduce-scatter.12
  654.8 44.9 all-gather.19
  704.1 75.5 reduce-scatter.20
  783.5 74.5 reduce-scatter.22
  862.1 57.0 reduce-scatter.18
  923.5 66.9 reduce-scatter.16
  993.3 25.0 reduce-scatter.14
